TPU v7x, 256 devices: a whole 4x4x8 slice. The times are simulated.
256 devices in a mesh: dop: 64 (over y, z, core), rng: 4 (over x).
Axes of the slice: x: 4, y: 4, z: 8, core: 2. Of those that a mesh axis runs over, the one named last changes fastest.
Arguments:
- raw_echo: float32 [2, 512, 512, 128], P(None, 'dop', 'rng'), may hold values from -6 to 6
- replica: float32 [2, 64], replicated, may hold values from -0.5 to 0.5
- beam_weights: bfloat16 [2, 512, 192], replicated, may hold values from -0.1875 to 0.1875
- pivots: int32 [128, 192], replicated, may hold values from 0 to 191, each once within a row
- owner_counts: int32 [64], replicated, may hold values from 1 to 4, 128 in all
- train_gates: int32 [128, 256], P(None, 'rng'), may hold values from 0 to 511, as said below
Outputs:
- factor: float32 [256, 384, 384], P('dop', 'rng')
Inputs may be any that keep to these rules, and one draw needn't show every extreme that they name: Owner o holds the run of owner_counts[o] consecutive Doppler bins that follows the bins of the owners below it; the counts sum to 128, and the largest is exactly 4 in every draw. `pivots`: each row is a permutation of 0 to 191. `train_gates`: in each row, columns r * 64 to (r + 1) * 64 - 1 hold distinct gates of range block r, that is of r * 128 to (r + 1) * 128 - 1.
All inputs are finite; a program needn't handle non-finite values.
Results may differ from a plain program's by a relative error of at most 0.005.
Values may be sent and summed in bfloat16 or wider, within the bound.
A program may use at most 64 MiB of HBM per device.

v0:
```python
import functools
import math

import jax
import jax.numpy as jnp
import numpy as np
from jax import lax
from jax.experimental import pallas as pl
from jax.experimental.pallas import tpu as pltpu
from jax.sharding import PartitionSpec as P

LOADING = 0.25
MESH = pl.DeviceIdType.MESH
BF16 = jnp.bfloat16
F32 = jnp.float32


def doppler_table(pulse_count):
    index = np.arange(pulse_count, dtype=np.int32)
    phase = (index[:, None] * index[None, :]) % pulse_count
    angle = phase.astype(np.float32) * np.float32(2.0 * math.pi / pulse_count)
    scale = np.float32(1.0 / math.sqrt(pulse_count))
    cos, sin = np.cos(angle) * scale, np.sin(angle) * scale
    table = np.block([[cos, -sin], [sin, cos]]).astype(np.float32)
    high = table.astype(BF16)
    low = (table - high.astype(np.float32)).astype(BF16)
    return high, low


def halves(x):
    high = x.astype(BF16)
    return high, (x - high.astype(F32)).astype(BF16)


def dot(a, b, dims=((1,), (0,))):
    return lax.dot_general(a, b, (dims, ((), ())), preferred_element_type=F32)


def front_kernel(most, counts_ref, raw_ref, rim_ref, replica_ref, high_ref, low_ref, gates_ref, out_ref, spec_ref, pick_ref):
    _, channels, gates, pulses = raw_ref.shape
    rim = rim_ref.shape[2]
    taps = replica_ref.shape[1]
    chosen = gates_ref.shape[1]
    owners = out_ref.shape[0]
    table_high, table_low = high_ref[...], low_ref[...]

    local = gates_ref[...] % gates
    pick_ref[...] = jnp.concatenate([local, local], axis=1)

    lane = lax.broadcasted_iota(jnp.int32, (gates, gates), 1)
    row = lax.broadcasted_iota(jnp.int32, (gates, gates), 0)
    back = (gates - lane[:8]) % gates
    rolled = []
    for part in range(2):
        line = jnp.concatenate([replica_ref[part : part + 1], jnp.zeros((1, gates - taps), F32)], axis=1)
        line = jnp.take_along_axis(jnp.broadcast_to(line, (8, gates)), back, axis=1)
        rolled.append(pltpu.roll(jnp.broadcast_to(line[:1], (gates, gates)), 0, 1, stride=1, stride_axis=0))
    near = (row >= lane) & (row - lane < taps)
    far = (row[:rim] + gates - lane[:rim]) < taps
    re_near, im_near = [jnp.where(near, part, 0.0) for part in rolled]
    re_far, im_far = [jnp.where(far, part[:rim], 0.0) for part in rolled]
    response = jnp.concatenate(
        [
            jnp.concatenate([re_near, -im_near], axis=1),
            jnp.concatenate([im_near, re_near], axis=1),
            jnp.concatenate([re_far, -im_far], axis=1),
            jnp.concatenate([im_far, re_far], axis=1),
        ],
        axis=0,
    )
    resp_high, resp_low = halves(response)

    for c in range(channels):
        high, low = halves(jnp.concatenate([raw_ref[0, c], raw_ref[1, c]], axis=1))
        inner = dot(high, table_high) + (dot(low, table_high) + dot(high, table_low))
        edge = jnp.concatenate([rim_ref[0, c], rim_ref[1, c]], axis=1)
        outer = dot(edge, table_high) + dot(edge, table_low)
        stacked = jnp.concatenate(
            [inner[:, :pulses], inner[:, pulses:], outer[:, :pulses], outer[:, pulses:]], axis=0
        )
        high, low = halves(stacked)
        tn = ((0,), (0,))
        done = dot(high, resp_high, tn) + (dot(low, resp_high, tn) + dot(high, resp_low, tn))
        spec_ref[:, c, :] = done[:, :gates]
        spec_ref[:, channels + c, :] = done[:, gates:]

    last_bin = pulses - 1
    first_half = lax.broadcasted_iota(jnp.int32, (channels, 2 * chosen), 1) < chosen

    def one_owner(owner, start):
        for slot in range(most):
            b = jnp.minimum(start + slot, last_bin)
            index = jnp.broadcast_to(pick_ref[pl.ds(b, 1), :], (channels, 2 * chosen))
            real = jnp.take_along_axis(spec_ref[b, :channels], index, axis=1)
            imag = jnp.take_along_axis(spec_ref[b, channels:], index, axis=1)
            out_ref[owner, slot] = jnp.where(first_half, real, imag).astype(BF16)
        return start + counts_ref[owner]

    lax.fori_loop(0, owners, one_owner, 0)


def front(raw, rim, replica, gates, counts, most):
    _, channels, gate_rows, pulses = raw.shape
    owners = counts.shape[0]
    high, low = doppler_table(pulses)
    vmem = pl.BlockSpec(memory_space=pltpu.VMEM)
    return pl.pallas_call(
        functools.partial(front_kernel, most),
        out_shape=jax.ShapeDtypeStruct((owners, most, channels, 2 * gates.shape[1]), BF16),
        in_specs=[pl.BlockSpec(memory_space=pltpu.SMEM)] + [vmem] * 6,
        out_specs=vmem,
        scratch_shapes=[
            pltpu.VMEM((pulses, 2 * channels, gate_rows), F32),
            pltpu.VMEM((pulses, 2 * gates.shape[1]), jnp.int32),
        ],
        name="front",
    )(counts, raw, rim, replica, jnp.asarray(high), jnp.asarray(low), gates)


def factor_panel(a_ref, r_ref, t, full, k):
    base, off = 128 * t, 8 * k
    order = a_ref.shape[1]
    tiles = order // 128 - t
    sub = lax.broadcasted_iota(jnp.int32, (8, 128), 0)
    lane = lax.broadcasted_iota(jnp.int32, (8, 128), 1)
    r0 = pl.multiple_of(base + off, 8)
    p = [a_ref[pl.ds(r0, 8), base + 128 * u : base + 128 * u + 128] for u in range(tiles)]
    cols = [jnp.take_along_axis(p[0], jnp.full((8, 128), off + j, jnp.int32), axis=1) for j in range(8)]
    s = {(i, j): jnp.broadcast_to(cols[j][i : i + 1], (8, 128)) for j in range(8) for i in range(j + 1)}
    rows = [[jnp.broadcast_to(p[u][j : j + 1], (8, 128)) for j in range(8)] for u in range(tiles)]
    for j in range(8):
        inv = lax.rsqrt(s[j, j])
        up = {m: s[j, m] * inv for m in range(j + 1, 8)}
        for i in range(j + 1, 8):
            for m in range(i, 8):
                s[i, m] = s[i, m] - up[i] * up[m]
        for u in range(tiles):
            rows[u][j] = rows[u][j] * inv
            for i in range(j + 1, 8):
                rows[u][i] = rows[u][i] - up[i] * rows[u][j]
    x = []
    for u in range(tiles):
        v = rows[u][0]
        for j in range(1, 8):
            v = jnp.where(sub == j, rows[u][j], v)
        if u == 0:
            v = jnp.where(lane >= off + sub, v, 0.0)
        x.append(v)
        r_ref[pl.ds(r0, 8), base + 128 * u : base + 128 * u + 128] = v * full
    x = jnp.concatenate(x, axis=1)
    high = x.astype(BF16).astype(F32)
    low = x - high
    pad = jnp.zeros_like(x)
    lhs = jnp.concatenate([high[:, :128], high[:, :128], low[:, :128], pad[:, :128]], axis=0).astype(BF16)
    rhs = jnp.concatenate([high, low, high, pad], axis=0).astype(BF16)
    a_ref[base : base + 128, base:] = a_ref[base : base + 128, base:] - dot(lhs, rhs, ((0,), (0,)))


def factor_trailing(a_ref, r_ref, t):
    base, end = 128 * t, 128 * t + 128
    high, low = halves(r_ref[base:end, end:])
    tn = ((0,), (0,))
    update = dot(high, high, tn) + (dot(low, high, tn) + dot(high, low, tn))
    a_ref[end:, end:] = a_ref[end:, end:] - update


def back_kernel(
    count_rows, sizes, counts_ref, src_ref, weights_ref, pivots_ref, out_ref,
    recv_ref, bsend_ref, brecv_ref, a_ref, r_ref,
    local_sem, send_sem, recv_sem, bsend_sem, brecv_sem, rsend_sem, rrecv_sem,
):
    ny, nz, nc, nx = sizes
    owners = ny * nz * nc
    dop, rng = lax.axis_index("dop"), lax.axis_index("rng")
    y, z, c = dop // (nz * nc), (dop // nc) % nz, dop % nc

    def peer(k):
        kc, kz, ky = k % nc, (k // nc) % nz, k // (nc * nz)
        return (((y + ky) % ny) * nz + (z + kz) % nz) * nc + (c + kc) % nc

    barrier = pltpu.get_barrier_semaphore()

    def greet(k, carry):
        pl.semaphore_signal(barrier, inc=1, device_id=(peer(k), rng), device_id_type=MESH)
        return carry

    lax.fori_loop(1, owners, greet, 0)
    for k in range(1, nx):
        pl.semaphore_signal(barrier, inc=1, device_id=(dop, (rng + k) % nx), device_id_type=MESH)
    pl.semaphore_wait(barrier, owners - 1 + nx - 1)

    def send(k, carry):
        other = peer(k)
        pltpu.make_async_remote_copy(
            src_ref=src_ref.at[other], dst_ref=recv_ref.at[dop], send_sem=send_sem, recv_sem=recv_sem,
            device_id=(other, rng), device_id_type=MESH,
        ).start()
        return carry

    lax.fori_loop(1, owners, send, 0)
    own = pltpu.make_async_copy(src_ref.at[dop], recv_ref.at[dop], local_sem)
    own.start()

    start = lax.fori_loop(0, owners, lambda o, total: total + jnp.where(o < dop, counts_ref[o], 0), 0)
    slot_bin = jnp.minimum(start + rng, pivots_ref.shape[0] - 1)
    full = jnp.where(rng < counts_ref[dop], 1.0, 0.0)
    dof = pivots_ref.shape[1]
    order = 2 * dof
    pivot = pivots_ref[pl.ds(slot_bin, 1), :]
    chooser = (lax.broadcasted_iota(jnp.int32, (dof, dof), 0) == jnp.broadcast_to(pivot, (dof, dof))).astype(BF16)
    r_ref[...] = jnp.zeros_like(r_ref)

    own.wait()
    others = recv_ref.at[pl.ds(0, owners - 1)]
    pltpu.make_async_copy(others, others, recv_sem).wait()
    pltpu.make_async_copy(others, others, send_sem).wait()

    w_real, w_imag = weights_ref[0], weights_ref[1]
    channels = w_real.shape[0]
    wide = recv_ref.shape[3]
    sign = jnp.where(lax.broadcasted_iota(jnp.int32, (dof, wide), 1) < wide // 2, 1.0, -1.0)
    tn = ((0,), (0,))
    for k in range(1, nx + 1):
        slot = (rng + k) % nx
        data = recv_ref[:, slot].reshape(channels, wide)
        beams = dot(w_real, data, tn) + sign * pltpu.roll(dot(w_imag, data, tn), wide // 2, 1)
        if k < nx:
            bsend_ref[k - 1] = beams.astype(BF16)
            pltpu.make_async_remote_copy(
                src_ref=bsend_ref.at[k - 1], dst_ref=brecv_ref.at[rng], send_sem=bsend_sem.at[k - 1],
                recv_sem=brecv_sem.at[k - 1], device_id=(dop, slot), device_id_type=MESH,
            ).start()
        else:
            brecv_ref[rng] = beams.astype(BF16)
    for k in range(1, nx):
        pltpu.make_async_copy(bsend_ref.at[k - 1], bsend_ref.at[k - 1], bsend_sem.at[k - 1]).wait()
        pltpu.make_async_copy(bsend_ref.at[k - 1], bsend_ref.at[k - 1], brecv_sem.at[k - 1]).wait()

    parts = []
    for k in range(nx):
        parts.append(dot(chooser, brecv_ref[k], tn))
    upper = jnp.concatenate(parts, axis=1)
    lower = jnp.concatenate([sign * pltpu.roll(part, wide // 2, 1) for part in parts], axis=1)
    both = jnp.concatenate([upper, lower], axis=0).astype(BF16)
    gram = dot(both, both, ((1,), (1,)))
    diagonal = lax.broadcasted_iota(jnp.int32, (order, order), 0) == lax.broadcasted_iota(jnp.int32, (order, order), 1)
    a_ref[...] = gram * (1.0 / count_rows) + jnp.where(diagonal, LOADING, 0.0)

    rows = order // nx

    def piece(r, ref):
        first = (rows * r) // 128 * 128
        return ref.at[:, first:] if first else ref

    def deliver(r):
        @pl.when(rng != r)
        def _():
            pltpu.make_async_remote_copy(
                src_ref=piece(r, r_ref.at[pl.ds(rows * r, rows)]), dst_ref=piece(r, out_ref.at[rng]),
                send_sem=rsend_sem.at[r], recv_sem=rrecv_sem.at[rng],
                device_id=(dop, r), device_id_type=MESH,
            ).start()

    for r in range(nx):
        first = (rows * r) // 128 * 128
        if first:
            @pl.when(rng == r)
            def _():
                out_ref[:, :, :first] = jnp.zeros((nx, rows, first), F32)

    sent = 0
    for t in range(order // 128):
        k = 0
        while k < 16:
            stop = 16
            if sent < nx and rows * (sent + 1) <= 128 * t + 128:
                stop = (rows * (sent + 1) - 128 * t) // 8
            lax.fori_loop(k, stop, lambda i, carry: (factor_panel(a_ref, r_ref, t, full, i), carry)[1], 0)
            if 128 * t + 8 * stop == rows * (sent + 1):
                deliver(sent)
                sent += 1
            k = stop
        if t + 1 < order // 128:
            factor_trailing(a_ref, r_ref, t)

    for r in range(nx):
        @pl.when(rng == r)
        def _():
            out_ref[r] = r_ref[rows * r : rows * r + rows]
            for s in range(nx):
                if s != r:
                    done = piece(r, out_ref.at[s])
                    pltpu.make_async_copy(done, done, rrecv_sem.at[s]).wait()

        @pl.when(rng != r)
        def _():
            left = piece(r, r_ref.at[pl.ds(rows * r, rows)])
            pltpu.make_async_copy(left, left, rsend_sem.at[r]).wait()


def back(outgoing, weights, pivots, counts, count_rows, sizes):
    owners, most, channels, wide = outgoing.shape
    nx = sizes[3]
    dof = pivots.shape[1]
    order = 2 * dof
    vmem = pl.BlockSpec(memory_space=pltpu.VMEM)
    dma = pltpu.SemaphoreType.DMA
    return pl.pallas_call(
        functools.partial(back_kernel, count_rows, sizes),
        out_shape=jax.ShapeDtypeStruct((most, order // nx, order), F32),
        in_specs=[pl.BlockSpec(memory_space=pltpu.SMEM)] + [vmem] * 3,
        out_specs=vmem,
        scratch_shapes=[
            pltpu.VMEM((owners, most, channels, wide), BF16),
            pltpu.VMEM((nx - 1, dof, wide), BF16),
            pltpu.VMEM((nx, dof, wide), BF16),
            pltpu.VMEM((order, order), F32),
            pltpu.VMEM((order, order), F32),
            dma, dma, dma, dma((nx - 1,)), dma((nx - 1,)), dma((nx,)), dma((nx,)),
        ],
        compiler_params=pltpu.CompilerParams(collective_id=1, has_side_effects=True),
        name="back",
    )(counts, outgoing, weights, pivots)


def shifted(array, axis, by):
    count = lax.axis_size(axis)
    pairs = [(i, i + by) for i in range(count) if 0 <= i + by < count]
    return lax.ppermute(array, axis, pairs)


def local(sizes, raw_echo, replica, beam_weights, pivots, owner_counts, train_gates):
    pulses = raw_echo.shape[3]
    taps = replica.shape[1]
    ranges = lax.axis_size("rng")
    most = 2 * (pulses // owner_counts.shape[0])
    rim = shifted(raw_echo[:, :, :taps, :].astype(BF16), "rng", -1)
    outgoing = front(raw_echo, rim, replica, train_gates, owner_counts, most)
    count_rows = float(train_gates.shape[1] * ranges)
    return back(outgoing, beam_weights, pivots, owner_counts, count_rows, sizes)


def solution(mesh):
    return jax.shard_map(
        functools.partial(local, (4, 8, 2, 4)),
        mesh=mesh,
        in_specs=(P(None, "dop", "rng", None), P(), P(), P(), P(), P(None, "rng")),
        out_specs=P("dop", "rng", None),
        check_vma=False,
    )
```

profile of v0, /device:TPU:38, one launch (start us, length us, event | category | flops | bytes accessed | tf_op | source)
XLA Modules:
  0.0 76.3 jit_solution(1427538543236343263)
XLA Ops:
  0.0 0.0 copy-start.3
  0.0 0.0 copy-start
  0.0 1.1 %slice.7 = bf16[2,8,64,128]{3,2,1,0:T(8,128)(2,1)S(1)} slice(f32[2,8,128,128]{3,2,1,0:T(8,128)} %raw_ref.1), slice={[0:2], [0:8], [0:64], [0:128]} | slice | bytes 524288 | tf_op jit(solution)/shard_map/slice | solution.py:337
  1.1 0.0 copy-start.2
  1.2 2.9 %collective-permute-start = (bf16[2,8,64,128]{3,2,1,0:T(8,128)(2,1)S(1)}, bf16[2,8,64,128]{3,2,1,0:T(8,128)(2,1)S(1)}, u32[]{:S(2)}, u32[]{:S(2)}) collective-permute-start(bf16[2,8,64,128]{3,2,1,0:T(8,128)(2,1)S(1)} %slice.7), channel_id=1, source_target_pairs={{1,0},{2,1},{3,2},{5,4},{6,5},{7,6},{9,8},{10,9},{11,10},{13,12},{... | collective-permute-start | bytes 786440 | tf_op jit(solution)/shard_map/ppermute | solution.py:329
  4.0 0.0 copy-done.3
  4.1 0.7 copy.9.gates_ref
  4.8 0.0 copy-done.2
  4.8 0.8 copy.11.pivots_ref
  5.5 0.0 copy-done
  5.5 1.0 %copy.10.weights_ref = bf16[2,512,192]{2,1,0:T(8,128)(2,1)} copy(bf16[2,512,192]{1,2,0:T(8,128)(2,1)S(1)} %copy-done) | data formatting | bytes 786432 | tf_op args[2]
  6.5 3.0 %collective-permute-done.rim_ref = bf16[2,8,64,128]{3,2,1,0:T(8,128)(2,1)S(1)} collective-permute-done((bf16[2,8,64,128]{3,2,1,0:T(8,128)(2,1)S(1)}, bf16[2,8,64,128]{3,2,1,0:T(8,128)(2,1)S(1)}, u32[]{:S(2)}, u32[]{:S(2)}) %collective-permute-start) | collective-permute-done | bytes 262176 | tf_op jit(solution)/shard_map/ppermute | solution.py:329
  9.6 0.0 copy-start.1
  9.6 0.7 copy-done.1
  10.3 10.1 %front.1.src_ref = bf16[64,4,8,128]{3,2,1,0:T(8,128)(2,1)} custom-call(s32[64]{0:T(128)} %counts_ref.3, f32[2,8,128,128]{3,2,1,0:T(8,128)} %raw_ref.1, bf16[2,8,64,128]{3,2,1,0:T(8,128)(2,1)} %copy-done.1, f32[2,64]{1,0:T(2,128)} %replica_ref.1, bf16[256,256]{1,0:T(8,128)(2,1)} %constant.4.clone.high_ref, bf16[256,256]{1,0:T(8,128)(2,1)} %constant.5.clone.low_ref, ...), custom_call_target="tpu_custom_call" | custom-call | tf_op jit(solution)/shard_map/front/pallas_call | solution.py:107
  20.3 54.0 %back.1 = f32[4,96,384]{2,1,0:T(8,128)} custom-call(s32[64]{0:T(128)} %counts_ref.3, bf16[64,4,8,128]{3,2,1,0:T(8,128)(2,1)} %front.1.src_ref, bf16[2,512,192]{2,1,0:T(8,128)(2,1)} %copy.10.weights_ref, s32[128,192]{1,0:T(8,128)} %copy.11.pivots_ref), custom_call_target="tpu_custom_call" | custom-call | tf_op jit(solution)/shard_map/back/pallas_call | solution.py:308
  74.4 1.9 %copy.13 = f32[4,96,384]{2,1,0:T(8,128)} copy(f32[4,96,384]{2,1,0:T(8,128)} %back.1) | data formatting | bytes 1179648
Async XLA Ops:
  0.0 4.0 %copy-start.3 = (s32[128,64]{0,1:T(8,128)S(1)}, s32[128,64]{0,1:T(8,128)}, u32[]{:S(2)}) copy-start(s32[128,64]{0,1:T(8,128)} %param.13) | copy-start | bytes 98308
  0.0 5.5 %copy-start = (bf16[2,512,192]{1,2,0:T(8,128)(2,1)S(1)}, bf16[2,512,192]{1,2,0:T(8,128)(2,1)}, u32[]{:S(2)}) copy-start(bf16[2,512,192]{1,2,0:T(8,128)(2,1)} %param.10) | copy-start | bytes 1179652
  1.1 3.6 %copy-start.2 = (s32[128,192]{0,1:T(8,128)S(1)}, s32[128,192]{0,1:T(8,128)}, u32[]{:S(2)}) copy-start(s32[128,192]{0,1:T(8,128)} %param.11) | copy-start | bytes 294916
  1.2 8.4 %collective-permute-start = (bf16[2,8,64,128]{3,2,1,0:T(8,128)(2,1)S(1)}, bf16[2,8,64,128]{3,2,1,0:T(8,128)(2,1)S(1)}, u32[]{:S(2)}, u32[]{:S(2)}) collective-permute-start(bf16[2,8,64,128]{3,2,1,0:T(8,128)(2,1)S(1)} %slice.7), channel_id=1, source_target_pairs={{1,0},{2,1},{3,2},{5,4},{6,5},{7,6},{9,8},{10,9},{11,10},{13,12},{... | collective-permute-start | bytes 786440 | tf_op jit(solution)/shard_map/ppermute | solution.py:329
  9.6 0.7 copy-start.1
where the time goes:
time: 77.3 us; the launch traced here: 76.3 us
  Pallas kernels  64.1 us (83%)
  local copies, waits for them, and re-layouts  6.23 us (8%)
  waiting for transfers between devices  3.04 us (4%)
  starting transfers between devices  2.88 us (4%)
    pallas_call x1, Pallas kernels, back(): pl.pallas_call(functools.partial(back_kernel, count_rows, sizes), out_sha...  54 us
    pallas_call x1, Pallas kernels, front(): pl.pallas_call(functools.partial(front_kernel, most), out_shape=jax.Shape...  10.1 us
    unnamed x12, local copies, waits for them, and re-layouts  5.1 us
    ppermute x1, waiting for transfers between devices, shifted(): return lax.ppermute(array, axis, pairs)  3.04 us
    ppermute x1, starting transfers between devices, shifted(): return lax.ppermute(array, axis, pairs)  2.88 us
  transfers between devices with their start and end apart: 1, of which 1 were waited for; matrix products, arithmetic and copies ran while one was open for 3% of the time, Pallas kernels for 0%

commit v1 on v0

v1 whole, which is shorter than its diff:
```python
import functools
import math

import jax
import jax.numpy as jnp
import numpy as np
from jax import lax
from jax.experimental import pallas as pl
from jax.experimental.pallas import tpu as pltpu
from jax.sharding import PartitionSpec as P

LOADING = 0.25
MESH = pl.DeviceIdType.MESH
BF16 = jnp.bfloat16
F32 = jnp.float32


def doppler_table(pulse_count):
    index = np.arange(pulse_count, dtype=np.int32)
    phase = (index[:, None] * index[None, :]) % pulse_count
    angle = phase.astype(np.float32) * np.float32(2.0 * math.pi / pulse_count)
    scale = np.float32(1.0 / math.sqrt(pulse_count))
    cos, sin = np.cos(angle) * scale, np.sin(angle) * scale
    table = np.block([[cos, -sin], [sin, cos]]).astype(np.float32)
    high = table.astype(BF16)
    low = (table - high.astype(np.float32)).astype(BF16)
    return high, low


def halves(x):
    high = x.astype(BF16)
    return high, (x - high.astype(F32)).astype(BF16)


def dot(a, b, dims=((1,), (0,))):
    return lax.dot_general(a, b, (dims, ((), ())), preferred_element_type=F32)


def factor_panel(a_ref, r_ref, t, full, k):
    base, off = 128 * t, 8 * k
    order = a_ref.shape[1]
    tiles = order // 128 - t
    sub = lax.broadcasted_iota(jnp.int32, (8, 128), 0)
    lane = lax.broadcasted_iota(jnp.int32, (8, 128), 1)
    r0 = pl.multiple_of(base + off, 8)
    p = [a_ref[pl.ds(r0, 8), base + 128 * u : base + 128 * u + 128] for u in range(tiles)]
    cols = [jnp.take_along_axis(p[0], jnp.full((8, 128), off + j, jnp.int32), axis=1) for j in range(8)]
    s = {(i, j): jnp.broadcast_to(cols[j][i : i + 1], (8, 128)) for j in range(8) for i in range(j + 1)}
    rows = [[jnp.broadcast_to(p[u][j : j + 1], (8, 128)) for j in range(8)] for u in range(tiles)]
    for j in range(8):
        inv = lax.rsqrt(s[j, j])
        up = {m: s[j, m] * inv for m in range(j + 1, 8)}
        for i in range(j + 1, 8):
            for m in range(i, 8):
                s[i, m] = s[i, m] - up[i] * up[m]
        for u in range(tiles):
            rows[u][j] = rows[u][j] * inv
            for i in range(j + 1, 8):
                rows[u][i] = rows[u][i] - up[i] * rows[u][j]
    x = []
    for u in range(tiles):
        v = rows[u][0]
        for j in range(1, 8):
            v = jnp.where(sub == j, rows[u][j], v)
        if u == 0:
            v = jnp.where(lane >= off + sub, v, 0.0)
        x.append(v)
        r_ref[pl.ds(r0, 8), base + 128 * u : base + 128 * u + 128] = v * full
    x = jnp.concatenate(x, axis=1)
    high = x.astype(BF16).astype(F32)
    low = x - high
    pad = jnp.zeros_like(x)
    lhs = jnp.concatenate([high[:, :128], high[:, :128], low[:, :128], pad[:, :128]], axis=0).astype(BF16)
    rhs = jnp.concatenate([high, low, high, pad], axis=0).astype(BF16)
    a_ref[base : base + 128, base:] = a_ref[base : base + 128, base:] - dot(lhs, rhs, ((0,), (0,)))


def factor_trailing(a_ref, r_ref, t):
    base, end = 128 * t, 128 * t + 128
    high, low = halves(r_ref[base:end, end:])
    tn = ((0,), (0,))
    update = dot(high, high, tn) + (dot(low, high, tn) + dot(high, low, tn))
    a_ref[end:, end:] = a_ref[end:, end:] - update


def filter_response(replica_ref, gates, rim):
    taps = replica_ref.shape[1]
    lane = lax.broadcasted_iota(jnp.int32, (gates, gates), 1)
    row = lax.broadcasted_iota(jnp.int32, (gates, gates), 0)
    back = (gates - lane[:8]) % gates
    rolled = []
    for part in range(2):
        line = jnp.concatenate([replica_ref[part : part + 1], jnp.zeros((1, gates - taps), F32)], axis=1)
        line = jnp.take_along_axis(jnp.broadcast_to(line, (8, gates)), back, axis=1)
        rolled.append(pltpu.roll(jnp.broadcast_to(line[:1], (gates, gates)), 0, 1, stride=1, stride_axis=0))
    near = (row >= lane) & (row - lane < taps)
    far = (row[:rim] + gates - lane[:rim]) < taps
    re_near, im_near = [jnp.where(near, part, 0.0) for part in rolled]
    re_far, im_far = [jnp.where(far, part[:rim], 0.0) for part in rolled]
    return (
        jnp.concatenate(
            [jnp.concatenate([re_near, -im_near], axis=1), jnp.concatenate([im_near, re_near], axis=1)], axis=0
        ),
        jnp.concatenate(
            [jnp.concatenate([re_far, -im_far], axis=1), jnp.concatenate([im_far, re_far], axis=1)], axis=0
        ),
    )


def kernel(
    count_rows, sizes, counts_ref, replica_ref, raw_hbm, high_hbm, low_hbm, weights_hbm, pivots_hbm, gates_hbm, out_ref,
    raw_ref, high_ref, low_ref, weights_ref, pivots_ref, gates_ref,
    rim_out_ref, rim_in_ref, part_ref, spec_ref, pick_ref, starts_ref,
    pack_ref, recv_ref, bsend_ref, brecv_ref, a_ref, r_ref,
    load_sem, rim_send_sem, rim_recv_sem, send_sem, recv_sem, bsend_sem, brecv_sem, rsend_sem, rrecv_sem,
):
    ny, nz, nc, nx = sizes
    owners = ny * nz * nc
    _, channels, gates, pulses = raw_ref.shape
    rim = rim_in_ref.shape[2]
    most, wide = pack_ref.shape[1], pack_ref.shape[3]
    dop, rng = lax.axis_index("dop"), lax.axis_index("rng")
    y, z, c = dop // (nz * nc), (dop // nc) % nz, dop % nc
    tn = ((0,), (0,))

    def owner_at(ky, kz, kc):
        return (((y + ky) % ny) * nz + (z + kz) % nz) * nc + (c + kc) % nc

    loads = [
        pltpu.make_async_copy(raw_hbm.at[:, :, :rim], raw_ref.at[:, :, :rim], load_sem.at[0]),
        pltpu.make_async_copy(high_hbm, high_ref, load_sem.at[1]),
        pltpu.make_async_copy(low_hbm, low_ref, load_sem.at[2]),
        pltpu.make_async_copy(raw_hbm.at[:, :, rim:], raw_ref.at[:, :, rim:], load_sem.at[3]),
        pltpu.make_async_copy(gates_hbm, gates_ref, load_sem.at[4]),
        pltpu.make_async_copy(pivots_hbm, pivots_ref, load_sem.at[5]),
        pltpu.make_async_copy(weights_hbm, weights_ref, load_sem.at[6]),
    ]
    for load in loads:
        load.start()

    barrier = pltpu.get_barrier_semaphore()
    for k in range(1, nx):
        pl.semaphore_signal(barrier, inc=1, device_id=(dop, (rng + k) % nx), device_id_type=MESH)

    def greet(k, carry):
        other = owner_at(k // (nc * nz), (k // nc) % nz, k % nc)
        pl.semaphore_signal(barrier, inc=1, device_id=(other, rng), device_id_type=MESH)
        return carry

    lax.fori_loop(1, owners, greet, 0)

    loads[0].wait()
    for ch in range(channels):
        for part in range(2):
            rim_out_ref[ch, part] = raw_ref[part, ch, :rim].astype(BF16)

    pl.semaphore_wait(barrier, owners - 1 + nx - 1)

    @pl.when(rng > 0)
    def _():
        for ch in range(channels):
            pltpu.make_async_remote_copy(
                src_ref=rim_out_ref.at[ch], dst_ref=rim_in_ref.at[ch], send_sem=rim_send_sem.at[ch],
                recv_sem=rim_recv_sem.at[ch], device_id=(dop, rng - 1), device_id_type=MESH,
            ).start()

    @pl.when(rng == nx - 1)
    def _():
        rim_in_ref[...] = jnp.zeros_like(rim_in_ref)

    near, far = filter_response(replica_ref, gates, rim)
    near_high, near_low = halves(near)
    far_high, far_low = halves(far)
    for load in loads[1:4]:
        load.wait()
    for ch in range(channels):
        high, low = halves(jnp.concatenate([raw_ref[0, ch], raw_ref[1, ch]], axis=1))
        inner = dot(high, high_ref[...]) + (dot(low, high_ref[...]) + dot(high, low_ref[...]))
        high, low = halves(jnp.concatenate([inner[:, :pulses], inner[:, pulses:]], axis=0))
        part_ref[ch] = dot(high, near_high, tn) + (dot(low, near_high, tn) + dot(high, near_low, tn))

    def run(owner, total):
        starts_ref[owner] = total
        return total + counts_ref[owner]

    lax.fori_loop(0, owners, run, 0)
    loads[4].wait()
    local = gates_ref[...].T % gates
    pick_ref[...] = jnp.concatenate([local, local], axis=1)

    for ch in range(channels):
        @pl.when(rng < nx - 1)
        def _():
            pltpu.make_async_copy(rim_in_ref.at[ch], rim_in_ref.at[ch], rim_recv_sem.at[ch]).wait()

        edge = jnp.concatenate([rim_in_ref[ch, 0], rim_in_ref[ch, 1]], axis=1)
        outer = dot(edge, high_ref[...]) + dot(edge, low_ref[...])
        high, low = halves(jnp.concatenate([outer[:, :pulses], outer[:, pulses:]], axis=0))
        done = dot(high, far_high, tn) + (dot(low, far_high, tn) + dot(high, far_low, tn))
        done = done + part_ref[ch]
        spec_ref[:, ch, :] = done[:, :gates]
        spec_ref[:, channels + ch, :] = done[:, gates:]

    first_half = lax.broadcasted_iota(jnp.int32, (channels, wide), 1) < wide // 2

    def pack(owner, ref):
        for slot in range(most):
            b = jnp.minimum(starts_ref[owner] + slot, pulses - 1)
            index = jnp.broadcast_to(pick_ref[pl.ds(b, 1), :], (channels, wide))
            real = jnp.take_along_axis(spec_ref[b, :channels], index, axis=1)
            imag = jnp.take_along_axis(spec_ref[b, channels:], index, axis=1)
            ref[owner, slot] = jnp.where(first_half, real, imag).astype(BF16)

    def send(owner):
        pltpu.make_async_remote_copy(
            src_ref=pack_ref.at[owner], dst_ref=recv_ref.at[dop], send_sem=send_sem, recv_sem=recv_sem,
            device_id=(owner, rng), device_id_type=MESH,
        ).start()

    steps = ny * nc
    for kz in sorted(range(nz), key=lambda k: (min(k, nz - k), k)):
        def at(i, kz=kz):
            return owner_at(i % ny, kz, i // ny)

        first = 0 if kz else 1
        pack(at(first), pack_ref)

        def one(i, carry):
            pack(at(i), pack_ref)
            send(at(i - 1))
            return carry

        lax.fori_loop(first + 1, steps, one, 0)
        send(at(steps - 1))
    pack(dop, recv_ref)

    loads[5].wait()
    loads[6].wait()
    dof = pivots_ref.shape[0]
    order = 2 * dof
    slot_bin = jnp.minimum(starts_ref[dop] + rng, pulses - 1)
    full = jnp.where(rng < counts_ref[dop], 1.0, 0.0)
    pivot = jnp.take_along_axis(pivots_ref[...], jnp.full(pivots_ref.shape, slot_bin, jnp.int32), axis=1)
    pivot = jnp.concatenate([pivot, pivot], axis=1)[:, :dof]
    chooser = (lax.broadcasted_iota(jnp.int32, (dof, dof), 1) == pivot).astype(BF16)
    r_ref[...] = jnp.zeros_like(r_ref)
    rows = order // nx
    for r in range(nx):
        first = (rows * r) // 128 * 128
        if first:
            @pl.when(rng == r)
            def _():
                out_ref[:, :, :first] = jnp.zeros((nx, rows, first), F32)

    others = recv_ref.at[pl.ds(0, owners - 1)]
    pltpu.make_async_copy(others, others, recv_sem).wait()

    sign = jnp.where(lax.broadcasted_iota(jnp.int32, (dof, wide), 1) < wide // 2, 1.0, -1.0)
    for k in range(1, nx + 1):
        slot = (rng + k) % nx
        data = recv_ref[:, slot].reshape(owners * channels, wide)
        beams = dot(weights_ref[0], data) + sign * pltpu.roll(dot(weights_ref[1], data), wide // 2, 1)
        if k < nx:
            bsend_ref[k - 1] = beams.astype(BF16)
            pltpu.make_async_remote_copy(
                src_ref=bsend_ref.at[k - 1], dst_ref=brecv_ref.at[rng], send_sem=bsend_sem.at[k - 1],
                recv_sem=brecv_sem.at[k - 1], device_id=(dop, slot), device_id_type=MESH,
            ).start()
        else:
            brecv_ref[rng] = beams.astype(BF16)
    for k in range(1, nx):
        pltpu.make_async_copy(bsend_ref.at[k - 1], bsend_ref.at[k - 1], brecv_sem.at[k - 1]).wait()

    parts = [dot(chooser, brecv_ref[k]) for k in range(nx)]
    upper = jnp.concatenate(parts, axis=1)
    lower = jnp.concatenate([sign * pltpu.roll(part, wide // 2, 1) for part in parts], axis=1)
    both = jnp.concatenate([upper, lower], axis=0).astype(BF16)
    gram = dot(both, both, ((1,), (1,)))
    diagonal = lax.broadcasted_iota(jnp.int32, (order, order), 0) == lax.broadcasted_iota(jnp.int32, (order, order), 1)
    a_ref[...] = gram * (1.0 / count_rows) + jnp.where(diagonal, LOADING, 0.0)

    def piece(r, ref):
        first = (rows * r) // 128 * 128
        return ref.at[:, first:] if first else ref

    def deliver(r):
        @pl.when(rng != r)
        def _():
            pltpu.make_async_remote_copy(
                src_ref=piece(r, r_ref.at[pl.ds(rows * r, rows)]), dst_ref=piece(r, out_ref.at[rng]),
                send_sem=rsend_sem.at[r], recv_sem=rrecv_sem.at[rng],
                device_id=(dop, r), device_id_type=MESH,
            ).start()

    sent = 0
    for t in range(order // 128):
        k = 0
        while k < 16:
            stop = 16
            if sent < nx and rows * (sent + 1) <= 128 * t + 128:
                stop = (rows * (sent + 1) - 128 * t) // 8
            lax.fori_loop(k, stop, lambda i, carry: (factor_panel(a_ref, r_ref, t, full, i), carry)[1], 0)
            if 128 * t + 8 * stop == rows * (sent + 1):
                deliver(sent)
                sent += 1
            k = stop
        if t + 1 < order // 128:
            factor_trailing(a_ref, r_ref, t)

    pltpu.make_async_copy(others, others, send_sem).wait()
    for k in range(1, nx):
        pltpu.make_async_copy(bsend_ref.at[k - 1], bsend_ref.at[k - 1], bsend_sem.at[k - 1]).wait()

    @pl.when(rng > 0)
    def _():
        for ch in range(channels):
            pltpu.make_async_copy(rim_out_ref.at[ch], rim_out_ref.at[ch], rim_send_sem.at[ch]).wait()

    for r in range(nx):
        @pl.when(rng == r)
        def _():
            out_ref[r] = r_ref[rows * r : rows * r + rows]
            for s in range(nx):
                if s != r:
                    done = piece(r, out_ref.at[s])
                    pltpu.make_async_copy(done, done, rrecv_sem.at[s]).wait()

        @pl.when(rng != r)
        def _():
            left = piece(r, r_ref.at[pl.ds(rows * r, rows)])
            pltpu.make_async_copy(left, left, rsend_sem.at[r]).wait()


def local(sizes, raw_echo, replica, beam_weights, pivots, owner_counts, train_gates):
    _, channels, gates, pulses = raw_echo.shape
    taps = replica.shape[1]
    owners = owner_counts.shape[0]
    nx = sizes[3]
    dof = pivots.shape[1]
    order = 2 * dof
    chosen = train_gates.shape[1]
    most = 2 * (pulses // owners)
    count_rows = float(chosen * nx)
    high, low = doppler_table(pulses)
    weights, pivots, picks = beam_weights.transpose(0, 2, 1), pivots.T, train_gates.T
    vmem, anywhere = pl.BlockSpec(memory_space=pltpu.VMEM), pl.BlockSpec(memory_space=pl.ANY)
    dma = pltpu.SemaphoreType.DMA
    return pl.pallas_call(
        functools.partial(kernel, count_rows, sizes),
        out_shape=jax.ShapeDtypeStruct((most, order // nx, order), F32),
        in_specs=[pl.BlockSpec(memory_space=pltpu.SMEM), vmem] + [anywhere] * 6,
        out_specs=vmem,
        scratch_shapes=[
            pltpu.VMEM(raw_echo.shape, F32),
            pltpu.VMEM(high.shape, BF16),
            pltpu.VMEM(low.shape, BF16),
            pltpu.VMEM(weights.shape, BF16),
            pltpu.VMEM(pivots.shape, jnp.int32),
            pltpu.VMEM(picks.shape, jnp.int32),
            pltpu.VMEM((channels, 2, taps, pulses), BF16),
            pltpu.VMEM((channels, 2, taps, pulses), BF16),
            pltpu.VMEM((channels, pulses, 2 * gates), F32),
            pltpu.VMEM((pulses, 2 * channels, gates), F32),
            pltpu.VMEM((pulses, 2 * chosen), jnp.int32),
            pltpu.SMEM((owners,), jnp.int32),
            pltpu.VMEM((owners, most, channels, 2 * chosen), BF16),
            pltpu.VMEM((owners, most, channels, 2 * chosen), BF16),
            pltpu.VMEM((nx - 1, dof, 2 * chosen), BF16),
            pltpu.VMEM((nx, dof, 2 * chosen), BF16),
            pltpu.VMEM((order, order), F32),
            pltpu.VMEM((order, order), F32),
            dma((7,)), dma((channels,)), dma((channels,)), dma, dma,
            dma((nx - 1,)), dma((nx - 1,)), dma((nx,)), dma((nx,)),
        ],
        compiler_params=pltpu.CompilerParams(collective_id=1, has_side_effects=True),
        name="factors",
    )(owner_counts, replica, raw_echo, jnp.asarray(high), jnp.asarray(low), weights, pivots, picks)


def solution(mesh):
    return jax.shard_map(
        functools.partial(local, (4, 8, 2, 4)),
        mesh=mesh,
        in_specs=(P(None, "dop", "rng", None), P(), P(), P(), P(), P(None, "rng")),
        out_specs=P("dop", "rng", None),
        check_vma=False,
    )
```

time: 77.3 us -> 65.1 us (0.84); the launches traced: 76.3 us -> 65 us
  local copies, waits for them, and re-layouts: 6.23 us -> 1.92 us
  waiting for transfers between devices: 3.04 us -> 0 us
  starting transfers between devices: 2.88 us -> 0 us
  Pallas kernels: 64.1 us -> 63.1 us
    unnamed x12 -> x1, local copies, waits for them, and re-layouts: 5.1 us -> 1.92 us
    ppermute x1 -> x0, waiting for transfers between devices: 3.04 us -> none  [shifted(): return lax.ppermute(array, axis, pairs)]
    ppermute x1 -> x0, starting transfers between devices: 2.88 us -> none  [shifted(): return lax.ppermute(array, axis, pairs)]
    slice x1 -> x0, local copies, waits for them, and re-layouts: 1.13 us -> none  [local(): rim = shifted(raw_echo[:, :, :taps, :].astype(BF16), 'rng', -1)]
    pallas_call x2 -> x1, Pallas kernels: 64.1 us -> 63.1 us  [local(): pl.pallas_call(functools.partial(kernel, count_rows, sizes), out_shape=ja...]
  transfers between devices with their start and end apart: 1 -> 0, of which waited for: 1 -> 0; matrix products, arithmetic and copies ran while one was open for 3% -> 0% of each run, Pallas kernels for 0% -> 0%
where the time goes in v1:
time: 65.1 us; the launch traced here: 65 us
  Pallas kernels  63.1 us (97%)
  local copies, waits for them, and re-layouts  1.92 us (3%)
    pallas_call x1, Pallas kernels, local(): pl.pallas_call(functools.partial(kernel, count_rows, sizes), out_shape=ja...  63.1 us
    unnamed x1, local copies, waits for them, and re-layouts  1.92 us

profile of v1, /device:TPU:38, one launch (start us, length us, event | category | flops | bytes accessed | tf_op | source)
XLA Modules:
  0.0 65.0 jit_solution(11088037083032448587)
XLA Ops:
  0.0 63.1 %factors.1 = f32[4,96,384]{2,1,0:T(8,128)} custom-call(s32[64]{0:T(128)} %counts_ref.1, f32[2,64]{1,0:T(2,128)} %replica_ref.1, f32[2,8,128,128]{3,2,1,0:T(8,128)} %raw_hbm.1, bf16[256,256]{1,0:T(8,128)(2,1)} %constant.4.clone.high_hbm, bf16[256,256]{1,0:T(8,128)(2,1)} %constant.5.clone.low_hbm, bf16[2,192,512]{2,1,0:T(8,128)(2,1)} %bitcast.3, ...), custom_call_target="tpu_custom_call" | custom-call | tf_op jit(solution)/shard_map/factors/pallas_call | solution.py:348
  63.1 1.9 %copy.10 = f32[4,96,384]{2,1,0:T(8,128)} copy(f32[4,96,384]{2,1,0:T(8,128)} %factors.1) | data formatting | bytes 1179648

commit v2 on v1

--- a/solution.py
+++ b/solution.py
@@ -36,51 +36,62 @@
     return lax.dot_general(a, b, (dims, ((), ())), preferred_element_type=F32)
 
 
-def factor_panel(a_ref, r_ref, t, full, k):
-    base, off = 128 * t, 8 * k
+def factor_rows(a_ref, r_ref, r0, full, span):
     order = a_ref.shape[1]
-    tiles = order // 128 - t
-    sub = lax.broadcasted_iota(jnp.int32, (8, 128), 0)
-    lane = lax.broadcasted_iota(jnp.int32, (8, 128), 1)
-    r0 = pl.multiple_of(base + off, 8)
-    p = [a_ref[pl.ds(r0, 8), base + 128 * u : base + 128 * u + 128] for u in range(tiles)]
-    cols = [jnp.take_along_axis(p[0], jnp.full((8, 128), off + j, jnp.int32), axis=1) for j in range(8)]
-    s = {(i, j): jnp.broadcast_to(cols[j][i : i + 1], (8, 128)) for j in range(8) for i in range(j + 1)}
-    rows = [[jnp.broadcast_to(p[u][j : j + 1], (8, 128)) for j in range(8)] for u in range(tiles)]
-    for j in range(8):
-        inv = lax.rsqrt(s[j, j])
-        up = {m: s[j, m] * inv for m in range(j + 1, 8)}
-        for i in range(j + 1, 8):
-            for m in range(i, 8):
-                s[i, m] = s[i, m] - up[i] * up[m]
+    edge = r0 // 128 * 128
+    tiles, groups = (order - edge) // 128, span // 8
+    shape = (8, 128)
+    sub = lax.broadcasted_iota(jnp.int32, shape, 0)
+    lane = lax.broadcasted_iota(jnp.int32, shape, 1)
+    p = [[a_ref[r0 + 8 * g : r0 + 8 * g + 8, edge + 128 * u : edge + 128 * u + 128] for u in range(tiles)] for g in range(groups)]
+
+    def column(v, m):
+        return jnp.broadcast_to(v[:, m : m + 1], shape)
+
+    def line(v, i):
+        return jnp.broadcast_to(v[i : i + 1], shape)
+
+    for k in range(groups):
+        off = r0 - edge + 8 * k
+        cols = {g: [column(p[g][0], off + m) for m in range(8)] for g in range(k, groups)}
+        pivots = None
+        for j in range(8):
+            head = cols[k][j]
+            pivot = line(head, j)
+            across = {m: line(cols[k][m], j) for m in range(j + 1, 8)}
+            rows = [line(p[k][u], j) for u in range(tiles)]
+            inv = lax.rsqrt(pivot)
+            inv2 = inv * inv
+            pivots = inv if j == 0 else jnp.where(sub == j, inv, pivots)
+            if j < 7:
+                first = head * across[j + 1]
+                cols[k][j + 1] = cols[k][j + 1] - first * inv2
+                scaled = head * inv2
+                for m in range(j + 2, 8):
+                    cols[k][m] = cols[k][m] - scaled * across[m]
+                below = jnp.where(sub > j, scaled, 0.0)
+                for u in range(tiles):
+                    p[k][u] = p[k][u] - below * rows[u]
+            for g in range(k + 1, groups):
+                scaled = cols[g][j] * inv2
+                for m in range(j + 1, 8):
+                    cols[g][m] = cols[g][m] - scaled * across[m]
+                for u in range(tiles):
+                    p[g][u] = p[g][u] - scaled * rows[u]
         for u in range(tiles):
-            rows[u][j] = rows[u][j] * inv
-            for i in range(j + 1, 8):
-                rows[u][i] = rows[u][i] - up[i] * rows[u][j]
-    x = []
-    for u in range(tiles):
-        v = rows[u][0]
-        for j in range(1, 8):
-            v = jnp.where(sub == j, rows[u][j], v)
-        if u == 0:
-            v = jnp.where(lane >= off + sub, v, 0.0)
-        x.append(v)
-        r_ref[pl.ds(r0, 8), base + 128 * u : base + 128 * u + 128] = v * full
-    x = jnp.concatenate(x, axis=1)
-    high = x.astype(BF16).astype(F32)
-    low = x - high
-    pad = jnp.zeros_like(x)
-    lhs = jnp.concatenate([high[:, :128], high[:, :128], low[:, :128], pad[:, :128]], axis=0).astype(BF16)
-    rhs = jnp.concatenate([high, low, high, pad], axis=0).astype(BF16)
-    a_ref[base : base + 128, base:] = a_ref[base : base + 128, base:] - dot(lhs, rhs, ((0,), (0,)))
-
-
-def factor_trailing(a_ref, r_ref, t):
-    base, end = 128 * t, 128 * t + 128
-    high, low = halves(r_ref[base:end, end:])
-    tn = ((0,), (0,))
-    update = dot(high, high, tn) + (dot(low, high, tn) + dot(high, low, tn))
-    a_ref[end:, end:] = a_ref[end:, end:] - update
+            v = p[k][u] * pivots
+            if u == 0:
+                v = jnp.where(lane >= off + sub, v, 0.0)
+            p[k][u] = v
+            r_ref[r0 + 8 * k : r0 + 8 * k + 8, edge + 128 * u : edge + 128 * u + 128] = v * full
+    rest = r0 + span
+    if rest < order:
+        start = rest // 128 * 128
+        x = jnp.concatenate([jnp.concatenate(p[g][(start - edge) // 128 :], axis=1) for g in range(groups)], axis=0)
+        high = x.astype(BF16)
+        low = (x - high.astype(F32)).astype(BF16)
+        update = dot(jnp.concatenate([high, high, low], axis=0), jnp.concatenate([high, low, high], axis=0), ((0,), (0,)))
+        a_ref[rest:, start:] = a_ref[rest:, start:] - update[rest - start:]
 
 
 def filter_response(replica_ref, gates, rim):
@@ -139,15 +150,11 @@
         load.start()
 
     barrier = pltpu.get_barrier_semaphore()
+    steps = [(ky, kz, kc) for ky in range(ny) for kz in range(nz) for kc in range(nc)][1:]
+    for step in sorted(steps, key=lambda k: -min(k[0], ny - k[0]) - min(k[1], nz - k[1])):
+        pl.semaphore_signal(barrier, inc=1, device_id=(owner_at(*step), rng), device_id_type=MESH)
     for k in range(1, nx):
         pl.semaphore_signal(barrier, inc=1, device_id=(dop, (rng + k) % nx), device_id_type=MESH)
-
-    def greet(k, carry):
-        other = owner_at(k // (nc * nz), (k // nc) % nz, k % nc)
-        pl.semaphore_signal(barrier, inc=1, device_id=(other, rng), device_id_type=MESH)
-        return carry
-
-    lax.fori_loop(1, owners, greet, 0)
 
     loads[0].wait()
     for ch in range(channels):
@@ -292,20 +299,11 @@
                 device_id=(dop, r), device_id_type=MESH,
             ).start()
 
-    sent = 0
-    for t in range(order // 128):
-        k = 0
-        while k < 16:
-            stop = 16
-            if sent < nx and rows * (sent + 1) <= 128 * t + 128:
-                stop = (rows * (sent + 1) - 128 * t) // 8
-            lax.fori_loop(k, stop, lambda i, carry: (factor_panel(a_ref, r_ref, t, full, i), carry)[1], 0)
-            if 128 * t + 8 * stop == rows * (sent + 1):
-                deliver(sent)
-                sent += 1
-            k = stop
-        if t + 1 < order // 128:
-            factor_trailing(a_ref, r_ref, t)
+    span = 32
+    for r0 in range(0, order, span):
+        factor_rows(a_ref, r_ref, r0, full, span)
+        if (r0 + span) % rows == 0:
+            deliver((r0 + span) // rows - 1)
 
     pltpu.make_async_copy(others, others, send_sem).wait()
     for k in range(1, nx):
@@ -347,7 +345,7 @@
     dma = pltpu.SemaphoreType.DMA
     return pl.pallas_call(
         functools.partial(kernel, count_rows, sizes),
-        out_shape=jax.ShapeDtypeStruct((most, order // nx, order), F32),
+        out_shape=pltpu.VMEM((most, order // nx, order), F32),
         in_specs=[pl.BlockSpec(memory_space=pltpu.SMEM), vmem] + [anywhere] * 6,
         out_specs=vmem,
         scratch_shapes=[

time: 65.1 us -> 55.9 us (0.86)
  Pallas kernels: 63.1 us -> 55 us
  local copies, waits for them, and re-layouts: 1.92 us -> 0.82 us
    pallas_call x1, Pallas kernels: 63.1 us -> 55 us  [local(): pl.pallas_call(functools.partial(kernel, count_rows, sizes), out_shape=pl...]
    unnamed x1, local copies, waits for them, and re-layouts: 1.92 us -> 0.82 us
where the time goes in v2:
time: 55.9 us; the launch traced here: 55.8 us
  Pallas kernels  55 us (98%)
  local copies, waits for them, and re-layouts  0.82 us (1%)
    pallas_call x1, Pallas kernels, local(): pl.pallas_call(functools.partial(kernel, count_rows, sizes), out_shape=pl...  55 us

profile of v2, /device:TPU:38, one launch (start us, length us, event | category | flops | bytes accessed | tf_op | source)
XLA Modules:
  0.0 55.8 jit_solution(6068111994476917192)
XLA Ops:
  0.0 55.0 %factors.1 = f32[4,96,384]{2,1,0:T(8,128)S(1)} custom-call(s32[64]{0:T(128)} %counts_ref.1, f32[2,64]{1,0:T(2,128)} %replica_ref.1, f32[2,8,128,128]{3,2,1,0:T(8,128)} %raw_hbm.1, bf16[256,256]{1,0:T(8,128)(2,1)} %constant.4.clone.high_hbm, bf16[256,256]{1,0:T(8,128)(2,1)} %constant.5.clone.low_hbm, bf16[2,192,512]{2,1,0:T(8,128)(2,1)} %bitcast.3, ...), custom_call_target="tpu_custom_call" | custom-call | tf_op jit(solution)/shard_map/factors/pallas_call | solution.py:346
  55.0 0.8 %copy.10 = f32[4,96,384]{2,1,0:T(8,128)} copy(f32[4,96,384]{2,1,0:T(8,128)S(1)} %factors.1) | data formatting | bytes 1179648

commit v3 on v2

--- a/solution.py
+++ b/solution.py
@@ -123,7 +123,7 @@
     raw_ref, high_ref, low_ref, weights_ref, pivots_ref, gates_ref,
     rim_out_ref, rim_in_ref, part_ref, spec_ref, pick_ref, starts_ref,
     pack_ref, recv_ref, bsend_ref, brecv_ref, a_ref, r_ref,
-    load_sem, rim_send_sem, rim_recv_sem, send_sem, recv_sem, bsend_sem, brecv_sem, rsend_sem, rrecv_sem,
+    load_sem, rim_send_sem, rim_recv_sem, send_sem, recv_sem, bsend_sem, brecv_sem, rsend_sem, rrecv_sem, wave_sem,
 ):
     ny, nz, nc, nx = sizes
     owners = ny * nz * nc
@@ -150,18 +150,32 @@
         load.start()
 
     barrier = pltpu.get_barrier_semaphore()
-    steps = [(ky, kz, kc) for ky in range(ny) for kz in range(nz) for kc in range(nc)][1:]
-    for step in sorted(steps, key=lambda k: -min(k[0], ny - k[0]) - min(k[1], nz - k[1])):
-        pl.semaphore_signal(barrier, inc=1, device_id=(owner_at(*step), rng), device_id_type=MESH)
+    along_y = [owner_at(k, 0, 0) for k in range(1, ny)]
+    near = along_y + [owner_at(0, 1, 0), owner_at(0, nz - 1, 0), owner_at(0, 0, 1)]
+    for other in near:
+        pl.semaphore_signal(barrier, inc=1, device_id=(other, rng), device_id_type=MESH)
     for k in range(1, nx):
         pl.semaphore_signal(barrier, inc=1, device_id=(dop, (rng + k) % nx), device_id_type=MESH)
+    waves = [
+        [owner_at(0, 1, 0), owner_at(0, nz - 1, 0)],
+        [owner_at(0, 2, 0), owner_at(0, nz - 2, 0)],
+        along_y,
+        [owner_at(0, 0, 1)],
+    ]
+
+    def wave(number):
+        for other in waves[number]:
+            pl.semaphore_signal(wave_sem.at[number], inc=1, device_id=(other, rng), device_id_type=MESH)
+
+    def wave_end(number):
+        pl.semaphore_wait(wave_sem.at[number], len(waves[number]))
 
     loads[0].wait()
     for ch in range(channels):
         for part in range(2):
             rim_out_ref[ch, part] = raw_ref[part, ch, :rim].astype(BF16)
 
-    pl.semaphore_wait(barrier, owners - 1 + nx - 1)
+    pl.semaphore_wait(barrier, len(near) + nx - 1)
 
     @pl.when(rng > 0)
     def _():
@@ -175,15 +189,21 @@
     def _():
         rim_in_ref[...] = jnp.zeros_like(rim_in_ref)
 
-    near, far = filter_response(replica_ref, gates, rim)
-    near_high, near_low = halves(near)
-    far_high, far_low = halves(far)
+    wave(0)
+
+    own, next_ = filter_response(replica_ref, gates, rim)
+    near_high, near_low = halves(own)
+    far_high, far_low = halves(next_)
     for load in loads[1:4]:
         load.wait()
     for ch in range(channels):
         high, low = halves(jnp.concatenate([raw_ref[0, ch], raw_ref[1, ch]], axis=1))
         inner = dot(high, high_ref[...]) + (dot(low, high_ref[...]) + dot(high, low_ref[...]))
         high, low = halves(jnp.concatenate([inner[:, :pulses], inner[:, pulses:]], axis=0))
+        if ch < len(waves):
+            wave_end(ch)
+            if ch + 1 < len(waves):
+                wave(ch + 1)
         part_ref[ch] = dot(high, near_high, tn) + (dot(low, near_high, tn) + dot(high, near_low, tn))
 
     def run(owner, total):
@@ -252,12 +272,13 @@
     chooser = (lax.broadcasted_iota(jnp.int32, (dof, dof), 1) == pivot).astype(BF16)
     r_ref[...] = jnp.zeros_like(r_ref)
     rows = order // nx
-    for r in range(nx):
-        first = (rows * r) // 128 * 128
+    span = 32
+    for r0 in range(0, order, span):
+        first = r0 // 128 * 128
         if first:
-            @pl.when(rng == r)
+            @pl.when(rng == r0 // rows)
             def _():
-                out_ref[:, :, :first] = jnp.zeros((nx, rows, first), F32)
+                out_ref[:, r0 % rows : r0 % rows + span, :first] = jnp.zeros((nx, span, first), F32)
 
     others = recv_ref.at[pl.ds(0, owners - 1)]
     pltpu.make_async_copy(others, others, recv_sem).wait()
@@ -286,24 +307,21 @@
     diagonal = lax.broadcasted_iota(jnp.int32, (order, order), 0) == lax.broadcasted_iota(jnp.int32, (order, order), 1)
     a_ref[...] = gram * (1.0 / count_rows) + jnp.where(diagonal, LOADING, 0.0)
 
-    def piece(r, ref):
-        first = (rows * r) // 128 * 128
-        return ref.at[:, first:] if first else ref
-
-    def deliver(r):
-        @pl.when(rng != r)
+    def source(r0):
+        return r_ref.at[r0 : r0 + span, r0 // 128 * 128 :]
+
+    def target(slot, r0):
+        return out_ref.at[slot, r0 % rows : r0 % rows + span, r0 // 128 * 128 :]
+
+    for r0 in range(0, order, span):
+        factor_rows(a_ref, r_ref, r0, full, span)
+
+        @pl.when(rng != r0 // rows)
         def _():
             pltpu.make_async_remote_copy(
-                src_ref=piece(r, r_ref.at[pl.ds(rows * r, rows)]), dst_ref=piece(r, out_ref.at[rng]),
-                send_sem=rsend_sem.at[r], recv_sem=rrecv_sem.at[rng],
-                device_id=(dop, r), device_id_type=MESH,
+                src_ref=source(r0), dst_ref=target(rng, r0), send_sem=rsend_sem.at[r0 // span],
+                recv_sem=rrecv_sem.at[rng, r0 % rows // span], device_id=(dop, r0 // rows), device_id_type=MESH,
             ).start()
-
-    span = 32
-    for r0 in range(0, order, span):
-        factor_rows(a_ref, r_ref, r0, full, span)
-        if (r0 + span) % rows == 0:
-            deliver((r0 + span) // rows - 1)
 
     pltpu.make_async_copy(others, others, send_sem).wait()
     for k in range(1, nx):
@@ -318,15 +336,16 @@
         @pl.when(rng == r)
         def _():
             out_ref[r] = r_ref[rows * r : rows * r + rows]
-            for s in range(nx):
-                if s != r:
-                    done = piece(r, out_ref.at[s])
-                    pltpu.make_async_copy(done, done, rrecv_sem.at[s]).wait()
+            for r0 in range(rows * r, rows * r + rows, span):
+                for slot in range(nx):
+                    if slot != r:
+                        done = target(slot, r0)
+                        pltpu.make_async_copy(done, done, rrecv_sem.at[slot, r0 % rows // span]).wait()
 
         @pl.when(rng != r)
         def _():
-            left = piece(r, r_ref.at[pl.ds(rows * r, rows)])
-            pltpu.make_async_copy(left, left, rsend_sem.at[r]).wait()
+            for r0 in range(rows * r, rows * r + rows, span):
+                pltpu.make_async_copy(source(r0), source(r0), rsend_sem.at[r0 // span]).wait()
 
 
 def local(sizes, raw_echo, replica, beam_weights, pivots, owner_counts, train_gates):
@@ -368,7 +387,8 @@
             pltpu.VMEM((order, order), F32),
             pltpu.VMEM((order, order), F32),
             dma((7,)), dma((channels,)), dma((channels,)), dma, dma,
-            dma((nx - 1,)), dma((nx - 1,)), dma((nx,)), dma((nx,)),
+            dma((nx - 1,)), dma((nx - 1,)), dma((order // 32,)), dma((nx, order // nx // 32)),
+            pltpu.SemaphoreType.REGULAR((4,)),
         ],
         compiler_params=pltpu.CompilerParams(collective_id=1, has_side_effects=True),
         name="factors",

time: 55.9 us -> 57.5 us (1.029)
  Pallas kernels: 55 us -> 56.4 us
    pallas_call x1, Pallas kernels: 55 us -> 56.4 us  [local(): pl.pallas_call(functools.partial(kernel, count_rows, sizes), out_shape=pl...]
where the time goes in v3:
time: 57.5 us; the launch traced here: 57.2 us
  Pallas kernels  56.4 us (98%)
  local copies, waits for them, and re-layouts  0.82 us (1%)
    pallas_call x1, Pallas kernels, local(): pl.pallas_call(functools.partial(kernel, count_rows, sizes), out_shape=pl...  56.4 us

profile of v3, /device:TPU:38, one launch (start us, length us, event | category | flops | bytes accessed | tf_op | source)
XLA Modules:
  0.0 57.2 jit_solution(2093770513739815489)
XLA Ops:
  0.0 56.4 %factors.1 = f32[4,96,384]{2,1,0:T(8,128)S(1)} custom-call(s32[64]{0:T(128)} %counts_ref.1, f32[2,64]{1,0:T(2,128)} %replica_ref.1, f32[2,8,128,128]{3,2,1,0:T(8,128)} %raw_hbm.1, bf16[256,256]{1,0:T(8,128)(2,1)} %constant.4.clone.high_hbm, bf16[256,256]{1,0:T(8,128)(2,1)} %constant.5.clone.low_hbm, bf16[2,192,512]{2,1,0:T(8,128)(2,1)} %bitcast.3, ...), custom_call_target="tpu_custom_call" | custom-call | tf_op jit(solution)/shard_map/factors/pallas_call | solution.py:365
  56.4 0.8 %copy.10 = f32[4,96,384]{2,1,0:T(8,128)} copy(f32[4,96,384]{2,1,0:T(8,128)S(1)} %factors.1) | data formatting | bytes 1179648

commit v4 on v3

--- a/solution.py
+++ b/solution.py
@@ -46,14 +46,17 @@
     p = [[a_ref[r0 + 8 * g : r0 + 8 * g + 8, edge + 128 * u : edge + 128 * u + 128] for u in range(tiles)] for g in range(groups)]
 
     def column(v, m):
-        return jnp.broadcast_to(v[:, m : m + 1], shape)
+        return jnp.take_along_axis(v, jnp.full(shape, m, jnp.int32), axis=1)
 
     def line(v, i):
         return jnp.broadcast_to(v[i : i + 1], shape)
 
     for k in range(groups):
         off = r0 - edge + 8 * k
-        cols = {g: [column(p[g][0], off + m) for m in range(8)] for g in range(k, groups)}
+        cols = {g: [column(p[g][0], off + m) for m in range(8)] for g in range(k + 1, groups)}
+        cols[k] = ahead if k else [column(p[k][0], off + m) for m in range(8)]
+        if k + 1 < groups:
+            ahead = [column(p[k + 1][0], off + 8 + m) for m in range(8)]
         pivots = None
         for j in range(8):
             head = cols[k][j]
@@ -74,6 +77,9 @@
                     p[k][u] = p[k][u] - below * rows[u]
             for g in range(k + 1, groups):
                 scaled = cols[g][j] * inv2
+                if g == k + 1:
+                    for m in range(8):
+                        ahead[m] = ahead[m] - scaled * line(cols[g][j], m)
                 for m in range(j + 1, 8):
                     cols[g][m] = cols[g][m] - scaled * across[m]
                 for u in range(tiles):
@@ -200,10 +206,6 @@
         high, low = halves(jnp.concatenate([raw_ref[0, ch], raw_ref[1, ch]], axis=1))
         inner = dot(high, high_ref[...]) + (dot(low, high_ref[...]) + dot(high, low_ref[...]))
         high, low = halves(jnp.concatenate([inner[:, :pulses], inner[:, pulses:]], axis=0))
-        if ch < len(waves):
-            wave_end(ch)
-            if ch + 1 < len(waves):
-                wave(ch + 1)
         part_ref[ch] = dot(high, near_high, tn) + (dot(low, near_high, tn) + dot(high, near_low, tn))
 
     def run(owner, total):
@@ -215,7 +217,14 @@
     local = gates_ref[...].T % gates
     pick_ref[...] = jnp.concatenate([local, local], axis=1)
 
+    wave_end(0)
+    wave(1)
+
     for ch in range(channels):
+        if ch in (2, 4, 6):
+            wave_end(ch // 2)
+            if ch < 6:
+                wave(ch // 2 + 1)
         @pl.when(rng < nx - 1)
         def _():
             pltpu.make_async_copy(rim_in_ref.at[ch], rim_in_ref.at[ch], rim_recv_sem.at[ch]).wait()
@@ -273,12 +282,14 @@
     r_ref[...] = jnp.zeros_like(r_ref)
     rows = order // nx
     span = 32
-    for r0 in range(0, order, span):
-        first = r0 // 128 * 128
+    last = order - rows
+    pieces = [(lo, lo + rows) for lo in range(0, last, rows)] + [(lo, lo + span) for lo in range(last, order, span)]
+    for lo, hi in pieces:
+        first = lo // 128 * 128
         if first:
-            @pl.when(rng == r0 // rows)
+            @pl.when(rng == lo // rows)
             def _():
-                out_ref[:, r0 % rows : r0 % rows + span, :first] = jnp.zeros((nx, span, first), F32)
+                out_ref[:, lo % rows : lo % rows + hi - lo, :first] = jnp.zeros((nx, hi - lo, first), F32)
 
     others = recv_ref.at[pl.ds(0, owners - 1)]
     pltpu.make_async_copy(others, others, recv_sem).wait()
@@ -287,7 +298,8 @@
     for k in range(1, nx + 1):
         slot = (rng + k) % nx
         data = recv_ref[:, slot].reshape(owners * channels, wide)
-        beams = dot(weights_ref[0], data) + sign * pltpu.roll(dot(weights_ref[1], data), wide // 2, 1)
+        both = dot(weights_ref[...], data)
+        beams = both[:dof] + sign * pltpu.roll(both[dof:], wide // 2, 1)
         if k < nx:
             bsend_ref[k - 1] = beams.astype(BF16)
             pltpu.make_async_remote_copy(
@@ -307,21 +319,22 @@
     diagonal = lax.broadcasted_iota(jnp.int32, (order, order), 0) == lax.broadcasted_iota(jnp.int32, (order, order), 1)
     a_ref[...] = gram * (1.0 / count_rows) + jnp.where(diagonal, LOADING, 0.0)
 
-    def source(r0):
-        return r_ref.at[r0 : r0 + span, r0 // 128 * 128 :]
-
-    def target(slot, r0):
-        return out_ref.at[slot, r0 % rows : r0 % rows + span, r0 // 128 * 128 :]
+    def source(lo, hi):
+        return r_ref.at[lo:hi, lo // 128 * 128 :]
+
+    def target(slot, lo, hi):
+        return out_ref.at[slot, lo % rows : lo % rows + hi - lo, lo // 128 * 128 :]
 
     for r0 in range(0, order, span):
         factor_rows(a_ref, r_ref, r0, full, span)
-
-        @pl.when(rng != r0 // rows)
-        def _():
-            pltpu.make_async_remote_copy(
-                src_ref=source(r0), dst_ref=target(rng, r0), send_sem=rsend_sem.at[r0 // span],
-                recv_sem=rrecv_sem.at[rng, r0 % rows // span], device_id=(dop, r0 // rows), device_id_type=MESH,
-            ).start()
+        for number, (lo, hi) in enumerate(pieces):
+            if hi == r0 + span:
+                @pl.when(rng != lo // rows)
+                def _():
+                    pltpu.make_async_remote_copy(
+                        src_ref=source(lo, hi), dst_ref=target(rng, lo, hi), send_sem=rsend_sem.at[number],
+                        recv_sem=rrecv_sem.at[rng, lo % rows // span], device_id=(dop, lo // rows), device_id_type=MESH,
+                    ).start()
 
     pltpu.make_async_copy(others, others, send_sem).wait()
     for k in range(1, nx):
@@ -336,16 +349,18 @@
         @pl.when(rng == r)
         def _():
             out_ref[r] = r_ref[rows * r : rows * r + rows]
-            for r0 in range(rows * r, rows * r + rows, span):
-                for slot in range(nx):
-                    if slot != r:
-                        done = target(slot, r0)
-                        pltpu.make_async_copy(done, done, rrecv_sem.at[slot, r0 % rows // span]).wait()
-
-        @pl.when(rng != r)
+
+    for number, (lo, hi) in enumerate(pieces):
+        @pl.when(rng == lo // rows)
         def _():
-            for r0 in range(rows * r, rows * r + rows, span):
-                pltpu.make_async_copy(source(r0), source(r0), rsend_sem.at[r0 // span]).wait()
+            for slot in range(nx):
+                if slot != lo // rows:
+                    done = target(slot, lo, hi)
+                    pltpu.make_async_copy(done, done, rrecv_sem.at[slot, lo % rows // span]).wait()
+
+        @pl.when(rng != lo // rows)
+        def _():
+            pltpu.make_async_copy(source(lo, hi), source(lo, hi), rsend_sem.at[number]).wait()
 
 
 def local(sizes, raw_echo, replica, beam_weights, pivots, owner_counts, train_gates):
@@ -359,7 +374,8 @@
     most = 2 * (pulses // owners)
     count_rows = float(chosen * nx)
     high, low = doppler_table(pulses)
-    weights, pivots, picks = beam_weights.transpose(0, 2, 1), pivots.T, train_gates.T
+    weights = beam_weights.transpose(0, 2, 1).reshape(order, -1)
+    pivots, picks = pivots.T, train_gates.T
     vmem, anywhere = pl.BlockSpec(memory_space=pltpu.VMEM), pl.BlockSpec(memory_space=pl.ANY)
     dma = pltpu.SemaphoreType.DMA
     return pl.pallas_call(

time: 57.5 us -> 51.6 us (0.90)
  Pallas kernels: 56.4 us -> 50.3 us
    pallas_call x1, Pallas kernels: 56.4 us -> 50.3 us  [local(): pl.pallas_call(functools.partial(kernel, count_rows, sizes), out_shape=pl...]
where the time goes in v4:
time: 51.6 us; the launch traced here: 51.1 us
  Pallas kernels  50.3 us (97%)
  local copies, waits for them, and re-layouts  0.82 us (2%)
    pallas_call x1, Pallas kernels, local(): pl.pallas_call(functools.partial(kernel, count_rows, sizes), out_shape=pl...  50.3 us

profile of v4, /device:TPU:38, one launch (start us, length us, event | category | flops | bytes accessed | tf_op | source)
XLA Modules:
  0.0 51.1 jit_solution(4282606345537910300)
XLA Ops:
  0.0 50.3 %factors.1 = f32[4,96,384]{2,1,0:T(8,128)S(1)} custom-call(s32[64]{0:T(128)} %counts_ref.1, f32[2,64]{1,0:T(2,128)} %replica_ref.1, f32[2,8,128,128]{3,2,1,0:T(8,128)} %raw_hbm.1, bf16[256,256]{1,0:T(8,128)(2,1)} %constant.4.clone.high_hbm, bf16[256,256]{1,0:T(8,128)(2,1)} %constant.5.clone.low_hbm, bf16[384,512]{1,0:T(8,128)(2,1)} %bitcast.5, ...), custom_call_target="tpu_custom_call" | custom-call | tf_op jit(solution)/shard_map/factors/pallas_call | solution.py:381
  50.3 0.8 %copy.10 = f32[4,96,384]{2,1,0:T(8,128)} copy(f32[4,96,384]{2,1,0:T(8,128)S(1)} %factors.1) | data formatting | bytes 1179648

commit v5 on v4

--- a/solution.py
+++ b/solution.py
@@ -128,14 +128,16 @@
     count_rows, sizes, counts_ref, replica_ref, raw_hbm, high_hbm, low_hbm, weights_hbm, pivots_hbm, gates_hbm, out_ref,
     raw_ref, high_ref, low_ref, weights_ref, pivots_ref, gates_ref,
     rim_out_ref, rim_in_ref, part_ref, spec_ref, pick_ref, starts_ref,
-    pack_ref, recv_ref, bsend_ref, brecv_ref, a_ref, r_ref,
+    mixed_ref, pack_ref, recv_ref, bsend_ref, brecv_ref, a_ref, r_ref,
     load_sem, rim_send_sem, rim_recv_sem, send_sem, recv_sem, bsend_sem, brecv_sem, rsend_sem, rrecv_sem, wave_sem,
 ):
     ny, nz, nc, nx = sizes
     owners = ny * nz * nc
     _, channels, gates, pulses = raw_ref.shape
     rim = rim_in_ref.shape[2]
-    most, wide = pack_ref.shape[1], pack_ref.shape[3]
+    most, wide = 2 * pack_ref.shape[2], pack_ref.shape[4]
+    halves_sent = pack_ref.shape[0]
+    some = channels // halves_sent
     dop, rng = lax.axis_index("dop"), lax.axis_index("rng")
     y, z, c = dop // (nz * nc), (dop // nc) % nz, dop % nc
     tn = ((0,), (0,))
@@ -157,17 +159,13 @@
 
     barrier = pltpu.get_barrier_semaphore()
     along_y = [owner_at(k, 0, 0) for k in range(1, ny)]
-    near = along_y + [owner_at(0, 1, 0), owner_at(0, nz - 1, 0), owner_at(0, 0, 1)]
+    along_z = [owner_at(0, k, 0) for k in (2, nz - 2)]
+    near = along_y + along_z + [owner_at(0, 1, 0), owner_at(0, nz - 1, 0), owner_at(0, 0, 1)]
     for other in near:
         pl.semaphore_signal(barrier, inc=1, device_id=(other, rng), device_id_type=MESH)
     for k in range(1, nx):
         pl.semaphore_signal(barrier, inc=1, device_id=(dop, (rng + k) % nx), device_id_type=MESH)
-    waves = [
-        [owner_at(0, 1, 0), owner_at(0, nz - 1, 0)],
-        [owner_at(0, 2, 0), owner_at(0, nz - 2, 0)],
-        along_y,
-        [owner_at(0, 0, 1)],
-    ]
+    waves = [along_z, along_y, [owner_at(0, 0, 1)]]
 
     def wave(number):
         for other in waves[number]:
@@ -220,11 +218,22 @@
     wave_end(0)
     wave(1)
 
-    for ch in range(channels):
-        if ch in (2, 4, 6):
-            wave_end(ch // 2)
-            if ch < 6:
-                wave(ch // 2 + 1)
+    loads[6].wait()
+    dof = pivots_ref.shape[0]
+    order = 2 * dof
+    lane = lax.broadcasted_iota(jnp.int32, (dof, 128), 1)
+    is_real = lane % (2 * some) < some
+    for half in range(halves_sent):
+        index = lane // channels * channels + half * some + lane % some
+        for lo in range(0, weights_ref.shape[1], 128):
+            real = jnp.take_along_axis(weights_ref[:dof, lo : lo + 128].astype(F32), index, axis=1)
+            imag = jnp.take_along_axis(weights_ref[dof:, lo : lo + 128].astype(F32), index, axis=1)
+            mixed_ref[half, :dof, lo : lo + 128] = jnp.where(is_real, real, imag).astype(BF16)
+            mixed_ref[half, dof:, lo : lo + 128] = jnp.where(is_real, -imag, real).astype(BF16)
+
+    first_half = lax.broadcasted_iota(jnp.int32, (channels, wide), 1) < wide // 2
+
+    def finish(ch):
         @pl.when(rng < nx - 1)
         def _():
             pltpu.make_async_copy(rim_in_ref.at[ch], rim_in_ref.at[ch], rim_recv_sem.at[ch]).wait()
@@ -234,46 +243,49 @@
         high, low = halves(jnp.concatenate([outer[:, :pulses], outer[:, pulses:]], axis=0))
         done = dot(high, far_high, tn) + (dot(low, far_high, tn) + dot(high, far_low, tn))
         done = done + part_ref[ch]
-        spec_ref[:, ch, :] = done[:, :gates]
-        spec_ref[:, channels + ch, :] = done[:, gates:]
-
-    first_half = lax.broadcasted_iota(jnp.int32, (channels, wide), 1) < wide // 2
-
-    def pack(owner, ref):
-        for slot in range(most):
-            b = jnp.minimum(starts_ref[owner] + slot, pulses - 1)
-            index = jnp.broadcast_to(pick_ref[pl.ds(b, 1), :], (channels, wide))
-            real = jnp.take_along_axis(spec_ref[b, :channels], index, axis=1)
-            imag = jnp.take_along_axis(spec_ref[b, channels:], index, axis=1)
-            ref[owner, slot] = jnp.where(first_half, real, imag).astype(BF16)
-
-    def send(owner):
+        at = ch // some * channels + ch % some
+        spec_ref[:, at, :] = done[:, :gates]
+        spec_ref[:, at + some, :] = done[:, gates:]
+
+    def packed(half, owner):
+        pairs = []
+        for pair in range(most // 2):
+            picked = []
+            for slot in (2 * pair, 2 * pair + 1):
+                b = jnp.minimum(starts_ref[owner] + slot, pulses - 1)
+                index = jnp.broadcast_to(pick_ref[pl.ds(b, 1), :], (channels, wide))
+                picked.append(jnp.take_along_axis(spec_ref[b, half * channels : half * channels + channels], index, axis=1))
+            pairs.append(jnp.where(first_half, picked[0], picked[1]).astype(BF16))
+        return pairs
+
+    def store(half, owner, pairs, ref):
+        for pair in range(most // 2):
+            ref[half, owner, pair] = pairs[pair]
+
+    def send(half, owner):
         pltpu.make_async_remote_copy(
-            src_ref=pack_ref.at[owner], dst_ref=recv_ref.at[dop], send_sem=send_sem, recv_sem=recv_sem,
-            device_id=(owner, rng), device_id_type=MESH,
+            src_ref=pack_ref.at[half, owner], dst_ref=recv_ref.at[half, dop], send_sem=send_sem.at[half],
+            recv_sem=recv_sem.at[half], device_id=(owner, rng), device_id_type=MESH,
         ).start()
 
-    steps = ny * nc
-    for kz in sorted(range(nz), key=lambda k: (min(k, nz - k), k)):
-        def at(i, kz=kz):
-            return owner_at(i % ny, kz, i // ny)
-
-        first = 0 if kz else 1
-        pack(at(first), pack_ref)
-
-        def one(i, carry):
-            pack(at(i), pack_ref)
-            send(at(i - 1))
-            return carry
-
-        lax.fori_loop(first + 1, steps, one, 0)
-        send(at(steps - 1))
-    pack(dop, recv_ref)
+    away = sorted(range(nz), key=lambda k: (min(k, nz - k), k))
+    for half in range(halves_sent):
+        for ch in range(half * some, half * some + some):
+            finish(ch)
+            if ch in (1, 3):
+                wave_end(ch // 2 + 1)
+                if ch == 1:
+                    wave(2)
+        for kz in away:
+            group = [owner_at(ky, kz, kc) for kc in range(nc) for ky in range(ny)]
+            ready = [packed(half, owner) for owner in group]
+            for number, owner in enumerate(group):
+                store(half, owner, ready[number], recv_ref if kz == 0 and number == 0 else pack_ref)
+            for number, owner in enumerate(group):
+                if kz or number:
+                    send(half, owner)
 
     loads[5].wait()
-    loads[6].wait()
-    dof = pivots_ref.shape[0]
-    order = 2 * dof
     slot_bin = jnp.minimum(starts_ref[dop] + rng, pulses - 1)
     full = jnp.where(rng < counts_ref[dop], 1.0, 0.0)
     pivot = jnp.take_along_axis(pivots_ref[...], jnp.full(pivots_ref.shape, slot_bin, jnp.int32), axis=1)
@@ -291,23 +303,30 @@
             def _():
                 out_ref[:, lo % rows : lo % rows + hi - lo, :first] = jnp.zeros((nx, hi - lo, first), F32)
 
-    others = recv_ref.at[pl.ds(0, owners - 1)]
-    pltpu.make_async_copy(others, others, recv_sem).wait()
-
-    sign = jnp.where(lax.broadcasted_iota(jnp.int32, (dof, wide), 1) < wide // 2, 1.0, -1.0)
-    for k in range(1, nx + 1):
+    sums = None
+    for half in range(halves_sent):
+        others = recv_ref.at[half, pl.ds(0, owners - 1)]
+        pltpu.make_async_copy(others, others, recv_sem.at[half]).wait()
+        data = [recv_ref[half, :, pair].reshape(owners * channels, wide) for pair in range(most // 2)]
+        share = dot(mixed_ref[half], jnp.concatenate(data, axis=1))
+        sums = share if sums is None else sums + share
+    left = lax.broadcasted_iota(jnp.int32, (dof, wide), 1) < wide // 2
+    sign = jnp.where(left, 1.0, -1.0)
+    for slot in range(most):
+        lo = slot // 2 * wide
+        real, imag = sums[:dof, lo : lo + wide], sums[dof:, lo : lo + wide]
+        if slot % 2:
+            real = pltpu.roll(real, wide // 2, 1)
+        else:
+            imag = pltpu.roll(imag, wide // 2, 1)
+        bsend_ref[slot] = jnp.where(left, real, imag).astype(BF16)
+    for k in range(1, nx):
         slot = (rng + k) % nx
-        data = recv_ref[:, slot].reshape(owners * channels, wide)
-        both = dot(weights_ref[...], data)
-        beams = both[:dof] + sign * pltpu.roll(both[dof:], wide // 2, 1)
-        if k < nx:
-            bsend_ref[k - 1] = beams.astype(BF16)
-            pltpu.make_async_remote_copy(
-                src_ref=bsend_ref.at[k - 1], dst_ref=brecv_ref.at[rng], send_sem=bsend_sem.at[k - 1],
-                recv_sem=brecv_sem.at[k - 1], device_id=(dop, slot), device_id_type=MESH,
-            ).start()
-        else:
-            brecv_ref[rng] = beams.astype(BF16)
+        pltpu.make_async_remote_copy(
+            src_ref=bsend_ref.at[slot], dst_ref=brecv_ref.at[rng], send_sem=bsend_sem.at[k - 1],
+            recv_sem=brecv_sem.at[k - 1], device_id=(dop, slot), device_id_type=MESH,
+        ).start()
+    brecv_ref[rng] = bsend_ref[rng]
     for k in range(1, nx):
         pltpu.make_async_copy(bsend_ref.at[k - 1], bsend_ref.at[k - 1], brecv_sem.at[k - 1]).wait()
 
@@ -336,7 +355,9 @@
                         recv_sem=rrecv_sem.at[rng, lo % rows // span], device_id=(dop, lo // rows), device_id_type=MESH,
                     ).start()
 
-    pltpu.make_async_copy(others, others, send_sem).wait()
+    for half in range(halves_sent):
+        others = recv_ref.at[half, pl.ds(0, owners - 1)]
+        pltpu.make_async_copy(others, others, send_sem.at[half]).wait()
     for k in range(1, nx):
         pltpu.make_async_copy(bsend_ref.at[k - 1], bsend_ref.at[k - 1], bsend_sem.at[k - 1]).wait()
 
@@ -396,15 +417,16 @@
             pltpu.VMEM((pulses, 2 * channels, gates), F32),
             pltpu.VMEM((pulses, 2 * chosen), jnp.int32),
             pltpu.SMEM((owners,), jnp.int32),
-            pltpu.VMEM((owners, most, channels, 2 * chosen), BF16),
-            pltpu.VMEM((owners, most, channels, 2 * chosen), BF16),
-            pltpu.VMEM((nx - 1, dof, 2 * chosen), BF16),
+            pltpu.VMEM((2, order, weights.shape[1]), BF16),
+            pltpu.VMEM((2, owners, most // 2, channels, 2 * chosen), BF16),
+            pltpu.VMEM((2, owners, most // 2, channels, 2 * chosen), BF16),
+            pltpu.VMEM((nx, dof, 2 * chosen), BF16),
             pltpu.VMEM((nx, dof, 2 * chosen), BF16),
             pltpu.VMEM((order, order), F32),
             pltpu.VMEM((order, order), F32),
-            dma((7,)), dma((channels,)), dma((channels,)), dma, dma,
+            dma((7,)), dma((channels,)), dma((channels,)), dma((2,)), dma((2,)),
             dma((nx - 1,)), dma((nx - 1,)), dma((order // 32,)), dma((nx, order // nx // 32)),
-            pltpu.SemaphoreType.REGULAR((4,)),
+            pltpu.SemaphoreType.REGULAR((3,)),
         ],
         compiler_params=pltpu.CompilerParams(collective_id=1, has_side_effects=True),
         name="factors",

time: 51.6 us -> 48.5 us (0.940)
  the two profiles are of different devices: /device:TPU:38 before, /device:TPU:1 now
where the time goes in v5:
time: 48.5 us; the launch traced here: 48.4 us
  Pallas kernels  47.6 us (98%)
  local copies, waits for them, and re-layouts  0.82 us (2%)
    pallas_call x1, Pallas kernels, local(): pl.pallas_call(functools.partial(kernel, count_rows, sizes), out_shape=pl...  47.6 us

profile of v5, /device:TPU:1, one launch (start us, length us, event | category | flops | bytes accessed | tf_op | source)
XLA Modules:
  0.0 48.4 jit_solution(2479253615761183470)
XLA Ops:
  0.0 47.6 %factors.1 = f32[4,96,384]{2,1,0:T(8,128)S(1)} custom-call(s32[64]{0:T(128)} %counts_ref.1, f32[2,64]{1,0:T(2,128)} %replica_ref.1, f32[2,8,128,128]{3,2,1,0:T(8,128)} %raw_hbm.1, bf16[256,256]{1,0:T(8,128)(2,1)} %constant.4.clone.high_hbm, bf16[256,256]{1,0:T(8,128)(2,1)} %constant.5.clone.low_hbm, bf16[384,512]{1,0:T(8,128)(2,1)} %bitcast.5, ...), custom_call_target="tpu_custom_call" | custom-call | tf_op jit(solution)/shard_map/factors/pallas_call | solution.py:402
  47.6 0.8 %copy.10 = f32[4,96,384]{2,1,0:T(8,128)} copy(f32[4,96,384]{2,1,0:T(8,128)S(1)} %factors.1) | data formatting | bytes 1179648

commit v6 on v5

--- a/solution.py
+++ b/solution.py
@@ -129,7 +129,7 @@
     raw_ref, high_ref, low_ref, weights_ref, pivots_ref, gates_ref,
     rim_out_ref, rim_in_ref, part_ref, spec_ref, pick_ref, starts_ref,
     mixed_ref, pack_ref, recv_ref, bsend_ref, brecv_ref, a_ref, r_ref,
-    load_sem, rim_send_sem, rim_recv_sem, send_sem, recv_sem, bsend_sem, brecv_sem, rsend_sem, rrecv_sem, wave_sem,
+    load_sem, rim_load_sem, rim_send_sem, rim_recv_sem, send_sem, recv_sem, bsend_sem, brecv_sem, rsend_sem, rrecv_sem, wave_sem,
 ):
     ny, nz, nc, nx = sizes
     owners = ny * nz * nc
@@ -146,26 +146,30 @@
         return (((y + ky) % ny) * nz + (z + kz) % nz) * nc + (c + kc) % nc
 
     loads = [
-        pltpu.make_async_copy(raw_hbm.at[:, :, :rim], raw_ref.at[:, :, :rim], load_sem.at[0]),
-        pltpu.make_async_copy(high_hbm, high_ref, load_sem.at[1]),
-        pltpu.make_async_copy(low_hbm, low_ref, load_sem.at[2]),
-        pltpu.make_async_copy(raw_hbm.at[:, :, rim:], raw_ref.at[:, :, rim:], load_sem.at[3]),
-        pltpu.make_async_copy(gates_hbm, gates_ref, load_sem.at[4]),
-        pltpu.make_async_copy(pivots_hbm, pivots_ref, load_sem.at[5]),
-        pltpu.make_async_copy(weights_hbm, weights_ref, load_sem.at[6]),
+        pltpu.make_async_copy(high_hbm, high_ref, load_sem.at[0]),
+        pltpu.make_async_copy(low_hbm, low_ref, load_sem.at[1]),
+        pltpu.make_async_copy(raw_hbm.at[:, :, rim:], raw_ref.at[:, :, rim:], load_sem.at[2]),
+        pltpu.make_async_copy(gates_hbm, gates_ref, load_sem.at[3]),
+        pltpu.make_async_copy(pivots_hbm, pivots_ref, load_sem.at[4]),
+        pltpu.make_async_copy(weights_hbm, weights_ref, load_sem.at[5]),
     ]
-    for load in loads:
+    rims = [
+        pltpu.make_async_copy(raw_hbm.at[:, ch, :rim], raw_ref.at[:, ch, :rim], rim_load_sem.at[ch])
+        for ch in range(channels)
+    ]
+    for load in rims + loads:
         load.start()
 
     barrier = pltpu.get_barrier_semaphore()
     along_y = [owner_at(k, 0, 0) for k in range(1, ny)]
     along_z = [owner_at(0, k, 0) for k in (2, nz - 2)]
-    near = along_y + along_z + [owner_at(0, 1, 0), owner_at(0, nz - 1, 0), owner_at(0, 0, 1)]
+    near = [owner_at(k, 0, kc) for k in range(1, ny) for kc in range(nc)] + [owner_at(0, 0, 1)]
+    near += [owner_at(0, k, kc) for k in (1, 2, nz - 2, nz - 1) for kc in range(nc)]
     for other in near:
         pl.semaphore_signal(barrier, inc=1, device_id=(other, rng), device_id_type=MESH)
     for k in range(1, nx):
         pl.semaphore_signal(barrier, inc=1, device_id=(dop, (rng + k) % nx), device_id_type=MESH)
-    waves = [along_z, along_y, [owner_at(0, 0, 1)]]
+    waves = [along_z, along_y]
 
     def wave(number):
         for other in waves[number]:
@@ -174,31 +178,33 @@
     def wave_end(number):
         pl.semaphore_wait(wave_sem.at[number], len(waves[number]))
 
-    loads[0].wait()
-    for ch in range(channels):
-        for part in range(2):
-            rim_out_ref[ch, part] = raw_ref[part, ch, :rim].astype(BF16)
-
     pl.semaphore_wait(barrier, len(near) + nx - 1)
-
-    @pl.when(rng > 0)
-    def _():
-        for ch in range(channels):
+    wave(0)
+
+    def send_rim(ch):
+        @pl.when(rng > 0)
+        def _():
             pltpu.make_async_remote_copy(
                 src_ref=rim_out_ref.at[ch], dst_ref=rim_in_ref.at[ch], send_sem=rim_send_sem.at[ch],
                 recv_sem=rim_recv_sem.at[ch], device_id=(dop, rng - 1), device_id_type=MESH,
             ).start()
 
+    for ch in range(channels):
+        rims[ch].wait()
+        for part in range(2):
+            rim_out_ref[ch, part] = raw_ref[part, ch, :rim].astype(BF16)
+        if ch:
+            send_rim(ch - 1)
+    send_rim(channels - 1)
+
     @pl.when(rng == nx - 1)
     def _():
         rim_in_ref[...] = jnp.zeros_like(rim_in_ref)
 
-    wave(0)
-
     own, next_ = filter_response(replica_ref, gates, rim)
     near_high, near_low = halves(own)
     far_high, far_low = halves(next_)
-    for load in loads[1:4]:
+    for load in loads[:3]:
         load.wait()
     for ch in range(channels):
         high, low = halves(jnp.concatenate([raw_ref[0, ch], raw_ref[1, ch]], axis=1))
@@ -211,14 +217,14 @@
         return total + counts_ref[owner]
 
     lax.fori_loop(0, owners, run, 0)
-    loads[4].wait()
+    loads[3].wait()
     local = gates_ref[...].T % gates
     pick_ref[...] = jnp.concatenate([local, local], axis=1)
 
     wave_end(0)
     wave(1)
 
-    loads[6].wait()
+    loads[5].wait()
     dof = pivots_ref.shape[0]
     order = 2 * dof
     lane = lax.broadcasted_iota(jnp.int32, (dof, 128), 1)
@@ -272,11 +278,9 @@
     for half in range(halves_sent):
         for ch in range(half * some, half * some + some):
             finish(ch)
-            if ch in (1, 3):
-                wave_end(ch // 2 + 1)
-                if ch == 1:
-                    wave(2)
-        for kz in away:
+            if ch == 2:
+                wave_end(1)
+        for kz in away if half else away[::-1]:
             group = [owner_at(ky, kz, kc) for kc in range(nc) for ky in range(ny)]
             ready = [packed(half, owner) for owner in group]
             for number, owner in enumerate(group):
@@ -285,7 +289,7 @@
                 if kz or number:
                     send(half, owner)
 
-    loads[5].wait()
+    loads[4].wait()
     slot_bin = jnp.minimum(starts_ref[dop] + rng, pulses - 1)
     full = jnp.where(rng < counts_ref[dop], 1.0, 0.0)
     pivot = jnp.take_along_axis(pivots_ref[...], jnp.full(pivots_ref.shape, slot_bin, jnp.int32), axis=1)
@@ -320,7 +324,7 @@
         else:
             imag = pltpu.roll(imag, wide // 2, 1)
         bsend_ref[slot] = jnp.where(left, real, imag).astype(BF16)
-    for k in range(1, nx):
+    for k in sorted(range(1, nx), key=lambda k: -min(k, nx - k)):
         slot = (rng + k) % nx
         pltpu.make_async_remote_copy(
             src_ref=bsend_ref.at[slot], dst_ref=brecv_ref.at[rng], send_sem=bsend_sem.at[k - 1],
@@ -424,9 +428,9 @@
             pltpu.VMEM((nx, dof, 2 * chosen), BF16),
             pltpu.VMEM((order, order), F32),
             pltpu.VMEM((order, order), F32),
-            dma((7,)), dma((channels,)), dma((channels,)), dma((2,)), dma((2,)),
+            dma((6,)), dma((channels,)), dma((channels,)), dma((channels,)), dma((2,)), dma((2,)),
             dma((nx - 1,)), dma((nx - 1,)), dma((order // 32,)), dma((nx, order // nx // 32)),
-            pltpu.SemaphoreType.REGULAR((3,)),
+            pltpu.SemaphoreType.REGULAR((2,)),
         ],
         compiler_params=pltpu.CompilerParams(collective_id=1, has_side_effects=True),
         name="factors",

time: 48.5 us -> 47.3 us (0.975)
  the two profiles are of different devices: /device:TPU:1 before, /device:TPU:34 now
where the time goes in v6:
time: 47.3 us; the launch traced here: 47.2 us
  Pallas kernels  46.4 us (98%)
  local copies, waits for them, and re-layouts  0.82 us (2%)
    pallas_call x1, Pallas kernels, local(): pl.pallas_call(functools.partial(kernel, count_rows, sizes), out_shape=pl...  46.4 us

profile of v6, /device:TPU:34, one launch (start us, length us, event | category | flops | bytes accessed | tf_op | source)
XLA Modules:
  0.0 47.2 jit_solution(12287992456105295015)
XLA Ops:
  0.0 46.4 %factors.1 = f32[4,96,384]{2,1,0:T(8,128)S(1)} custom-call(s32[64]{0:T(128)} %counts_ref.1, f32[2,64]{1,0:T(2,128)} %replica_ref.1, f32[2,8,128,128]{3,2,1,0:T(8,128)} %raw_hbm.1, bf16[256,256]{1,0:T(8,128)(2,1)} %constant.4.clone.high_hbm, bf16[256,256]{1,0:T(8,128)(2,1)} %constant.5.clone.low_hbm, bf16[384,512]{1,0:T(8,128)(2,1)} %bitcast.5, ...), custom_call_target="tpu_custom_call" | custom-call | tf_op jit(solution)/shard_map/factors/pallas_call | solution.py:406
  46.4 0.8 %copy.10 = f32[4,96,384]{2,1,0:T(8,128)} copy(f32[4,96,384]{2,1,0:T(8,128)S(1)} %factors.1) | data formatting | bytes 1179648
